TPU v7x, 32 devices: a whole 2x2x4 slice. The times are simulated.
32 devices in a mesh: parts: 2 (over x), ctx: 16 (over z, y, core).
Axes of the slice: x: 2, y: 2, z: 4, core: 2. Of those that a mesh axis runs over, the one named last changes fastest.
Arguments:
- query_proj: bfloat16 [4096, 4096], P(('parts', 'ctx')), parts along dimension 0, may hold values from -6 to 6
- key_proj: bfloat16 [4096, 4096], P(('parts', 'ctx')), parts along dimension 0, may hold values from -6 to 6
- value_proj: bfloat16 [4096, 4096], P(('parts', 'ctx')), parts along dimension 0, may hold values from -6 to 6
- cotangent: bfloat16 [4096, 2048], P(('parts', 'ctx')), parts along dimension 0, may hold values from -6 to 6
- out_weight: bfloat16 [4096, 2048], P('ctx'), may hold values from -0.125 to 0.125
- filters: float32 [256, 2048], P('ctx'), may hold values from -1.2 to 1.2
Outputs:
- query_grad: float32 [4096, 4096], P(('parts', 'ctx')), parts along dimension 0
- key_grad: float32 [4096, 4096], P(('parts', 'ctx')), parts along dimension 0
- value_grad: float32 [4096, 4096], P(('parts', 'ctx')), parts along dimension 0
- filter_grad: float32 [512, 2048], P(('parts', 'ctx')), parts along dimension 0
There are 2 independent parts, one for each index of `parts`. A program takes and returns all parts, laid end to end along the dimension named above; an argument that names none is the same for every part. Nothing has to cross between parts.
All inputs are finite; a program needn't handle non-finite values.
Results may differ from a plain program's by a relative error of at most 0.005.
Values may be sent and summed in bfloat16 or wider, within the bound.
No kernel may reach another device: no remote copies, remote signals or barrier semaphores. Data moves between devices by JAX's collectives and lax.ppermute only.
A program may use at most 192 MiB of HBM per device.

v0:
```python
import math
import jax
import jax.numpy as jnp
from jax import lax
from jax.sharding import PartitionSpec as P

inner_len = 128


def dft_pair(size_count):
    index_row = jnp.arange(size_count, dtype=jnp.int32)
    phase = (index_row[:, None] * index_row[None, :] % size_count).astype(jnp.float32) * (
        -2.0 * math.pi / size_count
    )
    return (jnp.cos(phase), jnp.sin(phase))


def twist(spectrum, sign):
    outer_len = spectrum.shape[1]
    total = outer_len * inner_len
    outer_index = jnp.arange(outer_len, dtype=jnp.int32)[:, None, None]
    inner_index = jnp.arange(inner_len, dtype=jnp.int32)[None, None, :]
    phase = (outer_index * inner_index % total).astype(jnp.float32) * (-2.0 * math.pi / total)
    tw_real = jnp.cos(phase)
    tw_imag = jnp.sin(phase) * sign
    real_part = spectrum[0] * tw_real - spectrum[1] * tw_imag
    imag_part = spectrum[0] * tw_imag + spectrum[1] * tw_real
    return jnp.stack([real_part, imag_part])


def last_matrix(sign):
    last_real, last_imag = dft_pair(inner_len)
    last_imag = last_imag * sign
    return jnp.stack([jnp.stack([last_real, -last_imag]), jnp.stack([last_imag, last_real])])


def apply_last(spectrum, sign):
    return jnp.einsum(
        "qzcn,pqkn->pzck", spectrum, last_matrix(sign), precision=lax.Precision.HIGHEST
    )


def forward_spectrum(signal):
    half_rows = signal.shape[0]
    outer_len = 2 * half_rows
    lead_real, lead_imag = dft_pair(outer_len)
    lead = jnp.stack([lead_real[:, :half_rows], lead_imag[:, :half_rows]])
    spectrum = jnp.einsum("pzn,ncm->pzcm", lead, signal, precision=lax.Precision.HIGHEST)
    return apply_last(twist(spectrum, 1.0), 1.0)


def inverse_spectrum(spectrum, want_imag):
    outer_len = spectrum.shape[1]
    half_rows = outer_len // 2
    spectrum = twist(apply_last(spectrum, -1.0), -1.0)
    lead_real, lead_imag = dft_pair(outer_len)
    lead_real = lead_real[:half_rows]
    lead_imag = lead_imag[:half_rows]
    scale = 1.0 / (outer_len * inner_len)
    if want_imag:
        lead = jnp.stack([jnp.stack([lead_real, lead_imag]), jnp.stack([-lead_imag, lead_real])])
    else:
        lead = jnp.stack([lead_real, lead_imag])[None]
    return jnp.einsum("qzcm,pqtz->ptcm", spectrum, lead * scale, precision=lax.Precision.HIGHEST)


def to_blocks(array):
    seq_len, chans = array.shape
    return (
        array.astype(jnp.float32).reshape(seq_len // inner_len, inner_len, chans).transpose(0, 2, 1)
    )


def from_blocks(array):
    half_rows, chans, unused = array.shape
    return array.transpose(0, 2, 1).reshape(half_rows * inner_len, chans)


def channel_work(mixed, gated, filters):
    seq_len, chans = mixed.shape
    group_count = filters.shape[0]
    group_size = chans // group_count
    half_rows = seq_len // inner_len
    outer_len = 2 * half_rows
    split_shape = (2, outer_len, group_count, group_size, inner_len)
    mix_spec = forward_spectrum(to_blocks(mixed)).reshape(split_shape)
    gate_spec = forward_spectrum(to_blocks(gated)).reshape(split_shape)
    filter_blocks = filters.reshape(group_count, half_rows, inner_len).transpose(1, 0, 2)
    filt_spec = forward_spectrum(filter_blocks)[:, :, :, None, :]
    filt_real, filt_imag = (filt_spec[0], filt_spec[1])
    mix_real, mix_imag = (mix_spec[0], mix_spec[1])
    gate_real, gate_imag = (gate_spec[0], gate_spec[1])
    conv_real = filt_real * mix_real - filt_imag * mix_imag
    conv_imag = filt_real * mix_imag + filt_imag * mix_real
    corr_real = filt_real * gate_real + filt_imag * gate_imag
    corr_imag = filt_real * gate_imag - filt_imag * gate_real
    combined = jnp.stack([conv_real - corr_imag, conv_imag + corr_real]).reshape(
        2, outer_len, chans, inner_len
    )
    both = inverse_spectrum(combined, True)
    conv_out = from_blocks(both[0])
    mixed_grad = from_blocks(both[1])
    lag_real = jnp.sum(mix_real * gate_real + mix_imag * gate_imag, axis=2)
    lag_imag = jnp.sum(mix_real * gate_imag - mix_imag * gate_real, axis=2)
    lag_out = inverse_spectrum(jnp.stack([lag_real, lag_imag]), False)[0]
    filter_grad = lag_out.transpose(1, 0, 2).reshape(group_count, seq_len) * (
        group_size * seq_len
    ) ** (-0.5)
    return (conv_out, mixed_grad, filter_grad)


def rounded_product(left, right):
    product = (left.astype(jnp.float32) * right.astype(jnp.float32)).astype(jnp.bfloat16)
    return lax.optimization_barrier(product)


def per_device(query_proj, key_proj, value_proj, cotangent, out_weight, filters):
    grad_rows = jnp.einsum(
        "tj,cj->tc",
        cotangent,
        lax.all_gather(out_weight, "ctx", axis=0, tiled=True),
        preferred_element_type=jnp.float32,
    ).astype(jnp.bfloat16)
    query_cols, key_cols, value_cols, grad_cols = (
        lax.all_to_all(query_proj, "ctx", split_axis=1, concat_axis=0, tiled=True),
        lax.all_to_all(key_proj, "ctx", split_axis=1, concat_axis=0, tiled=True),
        lax.all_to_all(value_proj, "ctx", split_axis=1, concat_axis=0, tiled=True),
        lax.all_to_all(grad_rows, "ctx", split_axis=1, concat_axis=0, tiled=True),
    )
    mixed_cols = rounded_product(key_cols, value_cols)
    gated_cols = rounded_product(query_cols, grad_cols)
    conv_out, mixed_grad, filter_grad = channel_work(mixed_cols, gated_cols, filters)
    query_grad_cols = grad_cols.astype(jnp.float32) * conv_out
    query_grad, key_grad, value_grad = (
        lax.all_to_all(query_grad_cols, "ctx", split_axis=0, concat_axis=1, tiled=True),
        lax.all_to_all(
            mixed_grad * value_cols.astype(jnp.float32),
            "ctx",
            split_axis=0,
            concat_axis=1,
            tiled=True,
        ),
        lax.all_to_all(
            mixed_grad * key_cols.astype(jnp.float32),
            "ctx",
            split_axis=0,
            concat_axis=1,
            tiled=True,
        ),
    )
    return (query_grad, key_grad, value_grad, filter_grad)


def solution(mesh):
    placed = (
        P(("parts", "ctx"), None),
        P(("parts", "ctx"), None),
        P(("parts", "ctx"), None),
        P(("parts", "ctx"), None),
        P("ctx", None),
        P("ctx", None),
    )
    return jax.shard_map(
        per_device,
        mesh=mesh,
        in_specs=placed,
        out_specs=(
            P(("parts", "ctx"), None),
            P(("parts", "ctx"), None),
            P(("parts", "ctx"), None),
            P(("parts", "ctx"), None),
        ),
        check_vma=False,
    )
```

profile of v0, /device:TPU:13, one launch (start us, length us, event | category | flops | bytes accessed | tf_op | source)
XLA Modules:
  0.0 509.7 jit_solution(12436188474592288112)
XLA Ops:
  7.9 2.3 copy.98
  10.2 6.7 %all-to-all-start.1 = ((bf16[128,16,256]{0,2,1:T(8,128)(2,1)}), bf16[128,16,256]{0,2,1:T(8,128)(2,1)S(1)}, u32[]{:S(2)}, u32[]{:S(2)}) async-start(bf16[128,16,256]{0,2,1:T(8,128)(2,1)} %bitcast.30), calls=%async_computation.1 | async-start | bytes 2097152 | tf_op jit(solution)/shard_map/all_to_all | solution.py:126
  16.9 1.3 copy.100
  18.2 49.8 %all-to-all-done.1 = bf16[128,16,256]{0,2,1:T(8,128)(2,1)S(1)} async-done(((bf16[128,16,256]{0,2,1:T(8,128)(2,1)}), bf16[128,16,256]{0,2,1:T(8,128)(2,1)S(1)}, u32[]{:S(2)}, u32[]{:S(2)}) %all-to-all-start.1) | async-done | bytes 1048608 | tf_op jit(solution)/shard_map/all_to_all | solution.py:126
  68.0 4.0 all-to-all-start.2
  71.9 2.3 copy.107
  74.2 46.1 %all-to-all-done.2 = bf16[128,16,256]{0,2,1:T(8,128)(2,1)S(1)} async-done(((bf16[128,16,256]{0,2,1:T(8,128)(2,1)}), bf16[128,16,256]{0,2,1:T(8,128)(2,1)S(1)}, u32[]{:S(2)}, u32[]{:S(2)}) %all-to-all-start.2) | async-done | bytes 1048608 | tf_op jit(solution)/shard_map/all_to_all | solution.py:127
  120.3 7.1 %all-to-all-start.3 = ((bf16[128,16,256]{0,2,1:T(8,128)(2,1)}), bf16[128,16,256]{0,2,1:T(8,128)(2,1)}, u32[]{:S(2)}, u32[]{:S(2)}) async-start(bf16[128,16,256]{0,2,1:T(8,128)(2,1)} %bitcast.223), calls=%async_computation.3 | async-start | bytes 2097152 | tf_op jit(solution)/shard_map/all_to_all | solution.py:125
  129.2 57.2 %all-gather.2.cloned.1.call-done = bf16[4096,2048]{1,0:T(8,128)(2,1)} async-done(((bf16[256,2048]{1,0:T(8,128)(2,1)}), bf16[4096,2048]{1,0:T(8,128)(2,1)}) %all-gather.2.cloned.1.call-update) | async-done | bytes 16777232 | tf_op jit(solution)/shard_map/all_gather | solution.py:121
  186.4 12.4 %convolution_convert_fusion = bf16[128,4096]{1,0:T(8,128)(2,1)} fusion(bf16[128,2048]{1,0:T(8,128)(2,1)S(1)} %copy-done, bf16[4096,2048]{1,0:T(8,128)(2,1)} %all-gather.2.cloned.1.call-done), kind=kOutput, calls=%fused_computation.13 | convolution fusion | flops 2148007936 | bytes 18350080 | tf_op jit(solution)/shard_map/tj,cj->tc/dot_general | solution.py:118
  198.8 2.3 copy.145
  201.0 10.4 %all-to-all-start = ((bf16[128,16,256]{0,2,1:T(8,128)(2,1)}), bf16[128,16,256]{0,2,1:T(8,128)(2,1)}, u32[]{:S(2)}, u32[]{:S(2)}) async-start(bf16[128,16,256]{0,2,1:T(8,128)(2,1)} %bitcast.222), calls=%async_computation | async-start | bytes 2097152 | tf_op jit(solution)/shard_map/all_to_all | solution.py:128
  212.9 2.3 mul.851
  215.2 5.7 %copy.104 = f32[1,32,256,128]{2,3,1,0:T(8,128)} copy(f32[1,32,256,128]{3,2,1,0:T(8,128)} %bitcast.214) | data formatting | bytes 8388608 | tf_op jit(solution)/shard_map/mul | solution.py:93
  221.1 2.3 mul.862
  223.4 5.6 %copy.106 = f32[1,32,256,128]{2,3,1,0:T(8,128)} copy(f32[1,32,256,128]{3,2,1,0:T(8,128)} %bitcast.215) | data formatting | bytes 8388608 | tf_op jit(solution)/shard_map/mul | solution.py:93
  229.1 1.2 fusion.19
  230.8 5.6 %fusion.26 = f32[2,32,256,128]{3,1,2,0:T(8,128)} fusion(bf16[16,128,256]{1,0,2:T(8,128)(2,1)S(1)} %bitcast.218, f32[1,32,16]{2,1,0:T(8,128)S(1)} %get-tuple-element.47, f32[1,32,16]{2,1,0:T(8,128)S(1)} %get-tuple-element.48), kind=kOutput, calls=%fused_computation.48 | convolution fusion | flops 402654208 | bytes 9441280 | tf_op jit(solution)/shard_map/pzn,ncm->pzcm/dot_general | solution.py:48
  236.4 2.8 fusion.22
  239.7 3.4 fusion.24
  243.1 6.2 %multiply_subtract_fusion.3 = (f32[1,32,256,128]{3,1,2,0:T(8,128)}, f32[1,32,256,128]{3,1,2,0:T(8,128)}, f32[1,32,256,128]{3,1,2,0:T(8,128)S(1)}, f32[1,32,256,128]{3,1,2,0:T(8,128)}) fusion(f32[2,32,256,128]{3,1,2,0:T(8,128)S(1)} %bitcast.212, f32[32,128]{1,0:T(8,128)S(1)} %get-tuple-element.49, f32[32,128]{1,0:T(8,128)S(1)} %get-tuple-element.50, ...), kind=kLoop, calls=%fused_computation.23 | loop fusion | flops 12582912 | bytes 33587200 | tf_op jit(solution)/shard_map/sub | solution.py:26
  249.4 4.5 pad_maximum_fusion
  253.9 12.6 %fusion.9 = f32[2,32,256,128]{2,3,1,0:T(8,128)S(1)} fusion(f32[2,32,256,128]{3,1,2,0:T(8,128)S(1)} %pad_maximum_fusion, f32[1,2,128,128]{3,2,1,0:T(8,128)S(1)} %copy-done.6, f32[1,2,128,128]{3,2,1,0:T(8,128)S(1)} %copy-done.8), kind=kOutput, calls=%fused_computation.24 | convolution fusion | flops 6442516480 | bytes 17039360 | tf_op jit(solution)/shard_map/qzcn,pqkn->pzck/dot_general | solution.py:38
  266.5 3.2 pad_maximum_fusion.1
  269.7 16.7 %fusion.12 = f32[2,32,256,128]{2,3,1,0:T(8,128)} fusion(f32[2,32,256,128]{3,1,2,0:T(8,128)S(1)} %pad_maximum_fusion.1, f32[1,2,128,128]{3,2,1,0:T(8,128)S(1)} %copy-done.6, f32[1,2,128,128]{3,2,1,0:T(8,128)S(1)} %copy-done.8), kind=kOutput, calls=%fused_computation.25 | convolution fusion | flops 6442516480 | bytes 17039360 | tf_op jit(solution)/shard_map/qzcn,pqkn->pzck/dot_general | solution.py:38
  286.4 10.2 %multiply_add_fusion = (f32[1,32,256,128]{2,3,1,0:T(8,128)}, f32[1,32,256,128]{2,3,1,0:T(8,128)}, f32[1,32,256,128]{2,3,1,0:T(8,128)}, f32[1,32,256,128]{2,3,1,0:T(8,128)}) fusion(f32[2,32,256,128]{2,3,1,0:T(8,128)} %fusion.12, f32[2,32,256,128]{2,3,1,0:T(8,128)S(1)} %fusion.9, f32[1,32,256,128]{2,3,1,0:T(8,128)} %copy.106, f32[1,32,256,128]{2,3,1,0:T(8,128)S(1)} %copy-done.2), kind=kLoop, calls=%fused_computation.15 | loop fusion | flops 20971520 | bytes 41943040 | tf_op jit(solution)/shard_map/add | solution.py:103
  296.7 7.8 %maximum_bitcast_fusion = f32[2,32,256,128,1]{2,3,1,0,4:T(8,128)} fusion(f32[1,32,256,128]{2,3,1,0:T(8,128)} %get-tuple-element.20, f32[1,32,256,128]{2,3,1,0:T(8,128)} %get-tuple-element.21), kind=kLoop, calls=%fused_computation.2 | loop fusion | flops 2097152 | bytes 16777216 | tf_op jit(solution)/shard_map/stack | solution.py:97
  304.4 10.3 %copy.139 = f32[2,32,256,128,1]{3,1,0,2,4:T(8,128)} copy(f32[2,32,256,128,1]{2,3,1,0,4:T(8,128)} %maximum_bitcast_fusion) | data formatting | bytes 16777216 | tf_op jit(solution)/shard_map/stack | solution.py:97
  314.7 12.5 %convolution_bitcast_fusion = f32[2,32,256,128]{3,1,2,0:T(8,128)S(1)} fusion(f32[2,32,256,128,1]{3,1,0,2,4:T(8,128)} %copy.139, f32[1,2,128,128]{3,2,1,0:T(8,128)S(1)} %copy-done.11, f32[1,2,128,128]{3,2,1,0:T(8,128)S(1)} %copy-done.9), kind=kOutput, calls=%fused_computation.26 | convolution fusion | flops 6442516480 | bytes 17039360 | tf_op jit(solution)/shard_map/qzcn,pqkn->pzck/dot_general | solution.py:38
  327.2 1.3 multiply_subtract_fusion.1
  328.6 5.0 fusion.15
  333.6 5.3 %fusion.18 = (f32[16,128,256]{1,0,2:T(8,128)}, f32[16,128,256]{1,0,2:T(8,128)}, f32[16,128,256]{1,0,2:T(8,128)S(1)}) fusion(f32[2,16,256,128]{3,1,2,0:T(8,128)S(1)} %fusion.15, bf16[128,16,256]{0,2,1:T(8,128)(2,1)S(1)} %all-to-all-done.1, bf16[128,16,256]{0,2,1:T(8,128)(2,1)S(1)} %copy-done.4, bf16[128,16,256]{0,2,1:T(8,128)(2,1)} %all-to-all-done), kind=kLoop, calls=%fused_computation.33 | loop fusion | flops 3145728 | bytes 13631488 | tf_op jit(solution)/shard_map/mul | solution.py:144
  338.9 2.0 copy.120
  340.9 6.1 %all-to-all-start.4 = ((f32[16,128,256]{1,2,0:T(8,128)}), f32[16,128,256]{1,2,0:T(8,128)S(1)}, u32[]{:S(2)}, u32[]{:S(2)}) async-start(f32[16,128,256]{1,2,0:T(8,128)} %copy.120), calls=%async_computation.4 | async-start | bytes 4194304 | tf_op jit(solution)/shard_map/all_to_all | solution.py:135
  347.0 3.6 copy.121
  350.6 43.8 %all-to-all-done.4 = f32[16,128,256]{1,2,0:T(8,128)S(1)} async-done(((f32[16,128,256]{1,2,0:T(8,128)}), f32[16,128,256]{1,2,0:T(8,128)S(1)}, u32[]{:S(2)}, u32[]{:S(2)}) %all-to-all-start.4) | async-done | bytes 2097184 | tf_op jit(solution)/shard_map/all_to_all | solution.py:135
  394.4 4.9 all-to-all-start.5
  399.3 3.7 copy.122
  403.0 43.9 %all-to-all-done.5 = f32[16,128,256]{1,2,0:T(8,128)} async-done(((f32[16,128,256]{1,2,0:T(8,128)}), f32[16,128,256]{1,2,0:T(8,128)}, u32[]{:S(2)}, u32[]{:S(2)}) %all-to-all-start.5) | async-done | bytes 2097184 | tf_op jit(solution)/shard_map/all_to_all | solution.py:136
  446.8 5.3 %all-to-all-start.6 = ((f32[16,128,256]{1,2,0:T(8,128)}), f32[16,128,256]{1,2,0:T(8,128)}, u32[]{:S(2)}, u32[]{:S(2)}) async-start(f32[16,128,256]{1,2,0:T(8,128)} %copy.122), calls=%async_computation.6 | async-start | bytes 4194304 | tf_op jit(solution)/shard_map/all_to_all | solution.py:143
  452.1 5.6 %copy.125 = f32[1,32,256,128]{3,2,1,0:T(8,128)} copy(f32[1,32,256,128]{2,3,1,0:T(8,128)} %get-tuple-element.19) | data formatting | bytes 8388608 | tf_op jit(solution)/shard_map/sub | solution.py:104
  457.7 2.9 reduce_sum.19
  460.7 5.6 %copy.123 = f32[1,32,256,128]{3,2,1,0:T(8,128)} copy(f32[1,32,256,128]{2,3,1,0:T(8,128)} %get-tuple-element.18) | data formatting | bytes 8388608 | tf_op jit(solution)/shard_map/add | solution.py:103
  466.3 2.9 reduce_sum.18
  471.2 1.8 copy.128
  473.0 2.9 copy.129
  475.9 23.6 %all-to-all-done.6 = f32[16,128,256]{1,2,0:T(8,128)} async-done(((f32[16,128,256]{1,2,0:T(8,128)}), f32[16,128,256]{1,2,0:T(8,128)}, u32[]{:S(2)}, u32[]{:S(2)}) %all-to-all-start.6) | async-done | bytes 2097184 | tf_op jit(solution)/shard_map/all_to_all | solution.py:143
  499.5 2.9 copy.130
  (75 shorter events, 7.3 us)
Async XLA Ops:
  7.2 179.2 %copy-start = (bf16[128,2048]{1,0:T(8,128)(2,1)S(1)}, bf16[128,2048]{1,0:T(8,128)(2,1)}, u32[]{:S(2)}) copy-start(bf16[128,2048]{1,0:T(8,128)(2,1)} %param.9) | copy-start | bytes 1572868
  7.2 9.7 %copy-start.13 = (bf16[128,4096]{1,0:T(8,128)(2,1)S(1)}, bf16[128,4096]{1,0:T(8,128)(2,1)}, u32[]{:S(2)}) copy-start(bf16[128,4096]{1,0:T(8,128)(2,1)} %param.8) | copy-start | bytes 3145732
  7.2 179.2 %all-gather.2.cloned.1.call-start = ((), (), s32[]{:S(2)}) async-start(), calls=%async_computation.7 | async-start | bytes 17825792 | tf_op jit(solution)/shard_map/all_gather | solution.py:121
  10.2 64.0 %copy-start.14 = (f32[16,2048]{1,0:T(8,128)S(1)}, f32[16,2048]{1,0:T(8,128)}, u32[]{:S(2)}) copy-start(f32[16,2048]{1,0:T(8,128)} %param.11) | copy-start | bytes 393220
  10.2 57.8 %all-to-all-start.1 = ((bf16[128,16,256]{0,2,1:T(8,128)(2,1)}), bf16[128,16,256]{0,2,1:T(8,128)(2,1)S(1)}, u32[]{:S(2)}, u32[]{:S(2)}) async-start(bf16[128,16,256]{0,2,1:T(8,128)(2,1)} %bitcast.30), calls=%async_computation.1 | async-start | bytes 2097152 | tf_op jit(solution)/shard_map/all_to_all | solution.py:126
  68.0 52.3 %all-to-all-start.2 = ((bf16[128,16,256]{0,2,1:T(8,128)(2,1)}), bf16[128,16,256]{0,2,1:T(8,128)(2,1)S(1)}, u32[]{:S(2)}, u32[]{:S(2)}) async-start(bf16[128,16,256]{0,2,1:T(8,128)(2,1)} %bitcast.224), calls=%async_computation.2 | async-start | bytes 2097152 | tf_op jit(solution)/shard_map/all_to_all | solution.py:127
  120.3 108.8 %copy-start.3 = (bf16[128,16,256]{0,2,1:T(8,128)(2,1)}, bf16[128,16,256]{0,2,1:T(8,128)(2,1)S(1)}, u32[]{:S(2)}) copy-start(bf16[128,16,256]{0,2,1:T(8,128)(2,1)S(1)} %all-to-all-done.2) | copy-start | bytes 3145732
  120.3 80.8 %all-to-all-start.3 = ((bf16[128,16,256]{0,2,1:T(8,128)(2,1)}), bf16[128,16,256]{0,2,1:T(8,128)(2,1)}, u32[]{:S(2)}, u32[]{:S(2)}) async-start(bf16[128,16,256]{0,2,1:T(8,128)(2,1)} %bitcast.223), calls=%async_computation.3 | async-start | bytes 2097152 | tf_op jit(solution)/shard_map/all_to_all | solution.py:125
  129.2 82.9 %copy-start.5 = (f32[1,2,128,128]{3,2,1,0:T(8,128)}, f32[1,2,128,128]{3,2,1,0:T(8,128)S(1)}, u32[]{:S(2)}) copy-start(f32[1,2,128,128]{3,2,1,0:T(8,128)S(1)} %get-tuple-element.38) | copy-start | bytes 393220
  129.2 82.9 %copy-start.7 = (f32[1,2,128,128]{3,2,1,0:T(8,128)}, f32[1,2,128,128]{3,2,1,0:T(8,128)S(1)}, u32[]{:S(2)}) copy-start(f32[1,2,128,128]{3,2,1,0:T(8,128)S(1)} %get-tuple-element.39) | copy-start | bytes 393220
  201.0 35.4 %all-to-all-start = ((bf16[128,16,256]{0,2,1:T(8,128)(2,1)}), bf16[128,16,256]{0,2,1:T(8,128)(2,1)}, u32[]{:S(2)}, u32[]{:S(2)}) async-start(bf16[128,16,256]{0,2,1:T(8,128)(2,1)} %bitcast.222), calls=%async_computation | async-start | bytes 2097152 | tf_op jit(solution)/shard_map/all_to_all | solution.py:128
  229.0 7.4 %copy-start.15 = (f32[1,16,32]{2,1,0:T(8,128)}, f32[1,16,32]{2,1,0:T(8,128)S(1)}, u32[]{:S(2)}) copy-start(f32[1,16,32]{2,1,0:T(8,128)S(1)} %get-tuple-element.43) | copy-start | bytes 6148
  229.1 7.4 %copy-start.17 = (f32[1,16,32]{2,1,0:T(8,128)}, f32[1,16,32]{2,1,0:T(8,128)S(1)}, u32[]{:S(2)}) copy-start(f32[1,16,32]{2,1,0:T(8,128)S(1)} %get-tuple-element.55) | copy-start | bytes 6148
  239.5 3.6 slice-start
  239.7 3.4 slice-start.1
  249.4 4.5 copy-start.6
  249.4 4.5 copy-start.8
  269.7 16.7 %copy-start.2 = (f32[1,32,256,128]{2,3,1,0:T(8,128)S(1)}, f32[1,32,256,128]{2,3,1,0:T(8,128)}, u32[]{:S(2)}) copy-start(f32[1,32,256,128]{2,3,1,0:T(8,128)} %copy.104) | copy-start | bytes 12582916
  304.4 10.3 %copy-start.9 = (f32[1,2,128,128]{3,2,1,0:T(8,128)S(1)}, f32[1,2,128,128]{3,2,1,0:T(8,128)}, u32[]{:S(2)}) copy-start(f32[1,2,128,128]{3,2,1,0:T(8,128)} %get-tuple-element.37) | copy-start | bytes 393220
  304.4 10.3 %copy-start.11 = (f32[1,2,128,128]{3,2,1,0:T(8,128)S(1)}, f32[1,2,128,128]{3,2,1,0:T(8,128)}, u32[]{:S(2)}) copy-start(f32[1,2,128,128]{3,2,1,0:T(8,128)} %get-tuple-element.40) | copy-start | bytes 393220
  328.6 5.0 copy-start.4
  340.9 53.5 %all-to-all-start.4 = ((f32[16,128,256]{1,2,0:T(8,128)}), f32[16,128,256]{1,2,0:T(8,128)S(1)}, u32[]{:S(2)}, u32[]{:S(2)}) async-start(f32[16,128,256]{1,2,0:T(8,128)} %copy.120), calls=%async_computation.4 | async-start | bytes 4194304 | tf_op jit(solution)/shard_map/all_to_all | solution.py:135
  394.4 52.4 %all-to-all-start.5 = ((f32[16,128,256]{1,2,0:T(8,128)}), f32[16,128,256]{1,2,0:T(8,128)}, u32[]{:S(2)}, u32[]{:S(2)}) async-start(f32[16,128,256]{1,2,0:T(8,128)} %copy.121), calls=%async_computation.5 | async-start | bytes 4194304 | tf_op jit(solution)/shard_map/all_to_all | solution.py:136
  446.8 52.7 %all-to-all-start.6 = ((f32[16,128,256]{1,2,0:T(8,128)}), f32[16,128,256]{1,2,0:T(8,128)}, u32[]{:S(2)}, u32[]{:S(2)}) async-start(f32[16,128,256]{1,2,0:T(8,128)} %copy.122), calls=%async_computation.6 | async-start | bytes 4194304 | tf_op jit(solution)/shard_map/all_to_all | solution.py:143
  466.3 3.0 copy-start.10
  466.3 3.0 copy-start.12
  466.3 3.8 copy-start.16
  466.3 3.8 copy-start.18
  473.0 29.4 %copy-start.1 = (bf16[128,2048]{1,0:T(8,128)(2,1)S(1)}, bf16[128,2048]{1,0:T(8,128)(2,1)}, u32[]{:S(2)}) copy-start(bf16[128,2048]{1,0:T(8,128)(2,1)} %param.9) | copy-start | bytes 1572868
Sparse Core Ops, SparseCore 0:
  10.2 176.1 all-gather.1
where the time goes:
time: 516 us; the launch traced here: 510 us
  waiting for transfers between devices  265 us (51%)
  matrix products  70.3 us (14%)
  local copies, waits for them, and re-layouts  64.6 us (13%)
  other arithmetic  50.4 us (10%)
  starting transfers between devices  44.4 us (9%)
  between operations  14.9 us (3%)
    all_gather x1, waiting for transfers between devices, per_device(): lax.all_gather(out_weight, 'ctx', axis=0, tiled=True)  57.2 us
    all_to_all x1, waiting for transfers between devices, per_device(): lax.all_to_all(key_proj, 'ctx', split_axis=1, concat_axis=0, tiled=True)  49.8 us
    all_to_all x1, waiting for transfers between devices, per_device(): lax.all_to_all(value_proj, 'ctx', split_axis=1, concat_axis=0, tiled=True)  46.1 us
    all_to_all x1, waiting for transfers between devices, per_device(): lax.all_to_all(mixed_grad * value_cols.astype(jnp.float32), 'ctx', split_...  43.9 us
    all_to_all x1, waiting for transfers between devices, per_device(): lax.all_to_all(query_grad_cols, 'ctx', split_axis=0, concat_axis=1, tiled...  43.8 us
    dot_general x5, matrix products, apply_last(): jnp.einsum('qzcn,pqkn->pzck', spectrum, last_matrix(sign), precision=lax....  43 us
    all_to_all x1, waiting for transfers between devices, per_device(): lax.all_to_all(mixed_grad * key_cols.astype(jnp.float32), 'ctx', split_ax...  23.6 us
    mul x7, local copies, waits for them, and re-layouts, channel_work(): conv_real = filt_real * mix_real - filt_imag * mix_imag  16.2 us
  transfers between devices with their start and end apart: 8, of which 6 were waited for; matrix products, arithmetic and copies ran while one was open for 15% of the time, Pallas kernels for 0%

commit v1 on v0

--- a/solution.py
+++ b/solution.py
@@ -5,6 +5,19 @@
 from jax.sharding import PartitionSpec as P
 
 inner_len = 128
+
+
+def gather_around(x, axis, dim):
+    ways = lax.axis_size(axis)
+    up = [(d, (d + 1) % ways) for d in range(ways)]
+    down = [(d, (d - 1) % ways) for d in range(ways)]
+    earlier, later = ([x], [x])
+    for _ in range(ways // 2):
+        earlier.append(lax.ppermute(earlier[-1], axis, up))
+    for _ in range((ways - 1) // 2):
+        later.append(lax.ppermute(later[-1], axis, down))
+    line = jnp.concatenate([*earlier[::-1], *later[1:]], axis=dim)
+    return jnp.roll(line, (lax.axis_index(axis) - ways // 2) * x.shape[dim], axis=dim)
 
 
 def dft_pair(size_count):
@@ -118,7 +131,7 @@
     grad_rows = jnp.einsum(
         "tj,cj->tc",
         cotangent,
-        lax.all_gather(out_weight, "ctx", axis=0, tiled=True),
+        gather_around(out_weight, "ctx", 0),
         preferred_element_type=jnp.float32,
     ).astype(jnp.bfloat16)
     query_cols, key_cols, value_cols, grad_cols = (

time: 516 us -> 582 us (1.13)
  starting transfers between devices: 44.4 us -> 167 us
  waiting for transfers between devices: 265 us -> 165 us
  local copies, waits for them, and re-layouts: 64.6 us -> 121 us
  between operations: 14.9 us -> 1.78 us
    ppermute x0 -> x15, starting transfers between devices: none -> 115 us  [the longest x7 106 us: gather_around(): later.append(lax.ppermute(later[-1], axis, down))]
    unnamed x54 -> x155, local copies, waits for them, and re-layouts: 15.3 us -> 72.7 us
    all_gather x1 -> x0, waiting for transfers between devices: 57.2 us -> none  [per_device(): lax.all_gather(out_weight, 'ctx', axis=0, tiled=True)]
    all_to_all x1, waiting for transfers between devices: 46.1 us -> 5.15 us  [per_device(): lax.all_to_all(value_proj, 'ctx', split_axis=1, concat_axis=0, tiled=True)]
    all_to_all x1, waiting for transfers between devices: 49.8 us -> 11 us  [per_device(): lax.all_to_all(key_proj, 'ctx', split_axis=1, concat_axis=0, tiled=True)]
    ppermute x0 -> x15, waiting for transfers between devices: none -> 37.8 us  [the longest x8 23.9 us: gather_around(): earlier.append(lax.ppermute(earlier[-1], axis, up))]
    all_to_all x1, starting transfers between devices: 7.06 us -> 19.8 us  [per_device(): lax.all_to_all(query_proj, 'ctx', split_axis=1, concat_axis=0, tiled=True)]
  transfers between devices with their start and end apart: 8 -> 22, of which waited for: 6 -> 13; matrix products, arithmetic and copies ran while one was open for 15% -> 23% of each run, Pallas kernels for 0% -> 0%
where the time goes in v1:
time: 582 us; the launch traced here: 573 us
  starting transfers between devices  167 us (29%)
  waiting for transfers between devices  165 us (28%)
  local copies, waits for them, and re-layouts  121 us (21%)
  matrix products  67.3 us (12%)
  other arithmetic  51 us (9%)
    ppermute x7, starting transfers between devices, gather_around(): later.append(lax.ppermute(later[-1], axis, down))  106 us
    unnamed x155, local copies, waits for them, and re-layouts  72.7 us
    all_to_all x1, waiting for transfers between devices, per_device(): lax.all_to_all(mixed_grad * value_cols.astype(jnp.float32), 'ctx', split_...  43.9 us
    all_to_all x1, waiting for transfers between devices, per_device(): lax.all_to_all(query_grad_cols, 'ctx', split_axis=0, concat_axis=1, tiled...  43.8 us
    dot_general x5, matrix products, apply_last(): jnp.einsum('qzcn,pqkn->pzck', spectrum, last_matrix(sign), precision=lax....  43.1 us
    ppermute x8, waiting for transfers between devices, gather_around(): earlier.append(lax.ppermute(earlier[-1], axis, up))  23.9 us
    all_to_all x1, waiting for transfers between devices, per_device(): lax.all_to_all(mixed_grad * key_cols.astype(jnp.float32), 'ctx', split_ax...  23.5 us
    all_to_all x1, starting transfers between devices, per_device(): lax.all_to_all(query_proj, 'ctx', split_axis=1, concat_axis=0, tiled=True)  19.8 us
  transfers between devices with their start and end apart: 22, of which 13 were waited for; matrix products, arithmetic and copies ran while one was open for 23% of the time, Pallas kernels for 0%

profile of v1, /device:TPU:13, one launch (start us, length us, event | category | flops | bytes accessed | tf_op | source)
XLA Modules:
  0.0 573.0 jit_solution(5439214471979146351)
XLA Ops:
  2.5 12.1 %collective-permute-done = bf16[256,2048]{1,0:T(8,128)(2,1)S(1)} collective-permute-done((bf16[256,2048]{1,0:T(8,128)(2,1)}, bf16[256,2048]{1,0:T(8,128)(2,1)S(1)}, u32[]{:S(2)}, u32[]{:S(2)}) %collective-permute-start) | collective-permute-done | bytes 1048608 | tf_op jit(solution)/shard_map/ppermute | solution.py:16
  14.6 3.3 collective-permute-start.1
  17.9 11.8 %collective-permute-done.1 = bf16[256,2048]{1,0:T(8,128)(2,1)S(1)} collective-permute-done((bf16[256,2048]{1,0:T(8,128)(2,1)S(1)}, bf16[256,2048]{1,0:T(8,128)(2,1)S(1)}, u32[]{:S(2)}, u32[]{:S(2)}) %collective-permute-start.1) | collective-permute-done | bytes 1048608 | tf_op jit(solution)/shard_map/ppermute | solution.py:16
  29.6 3.4 collective-permute-start.2
  34.3 19.2 %collective-permute-start.9 = (bf16[256,2048]{1,0:T(8,128)(2,1)S(1)}, bf16[256,2048]{1,0:T(8,128)(2,1)S(1)}, u32[]{:S(2)}, u32[]{:S(2)}) collective-permute-start(bf16[256,2048]{1,0:T(8,128)(2,1)S(1)} %collective-permute-done.8), channel_id=1, source_target_pairs={{0,15},{1,0},{2,1},{3,2},{4,3},{5,4},{6,5},{7,6},{8,7},{9,8},{10,9... | collective-permute-start | bytes 3145736 | tf_op jit(solution)/shard_map/ppermute | solution.py:18
  55.7 21.2 %collective-permute-start.10 = (bf16[256,2048]{1,0:T(8,128)(2,1)S(1)}, bf16[256,2048]{1,0:T(8,128)(2,1)S(1)}, u32[]{:S(2)}, u32[]{:S(2)}) collective-permute-start(bf16[256,2048]{1,0:T(8,128)(2,1)S(1)} %collective-permute-done.9), channel_id=1, source_target_pairs={{0,15},{1,0},{2,1},{3,2},{4,3},{5,4},{6,5},{7,6},{8,7},{9,8},{10,9... | collective-permute-start | bytes 3145736 | tf_op jit(solution)/shard_map/ppermute | solution.py:18
  77.0 2.7 collective-permute-done.10
  80.7 22.7 %collective-permute-start.11 = (bf16[256,2048]{1,0:T(8,128)(2,1)S(1)}, bf16[256,2048]{1,0:T(8,128)(2,1)S(1)}, u32[]{:S(2)}, u32[]{:S(2)}) collective-permute-start(bf16[256,2048]{1,0:T(8,128)(2,1)S(1)} %collective-permute-done.10), channel_id=1, source_target_pairs={{0,15},{1,0},{2,1},{3,2},{4,3},{5,4},{6,5},{7,6},{8,7},{9,8},{10,9... | collective-permute-start | bytes 3145736 | tf_op jit(solution)/shard_map/ppermute | solution.py:18
  105.6 21.8 %collective-permute-start.12 = (bf16[256,2048]{1,0:T(8,128)(2,1)S(1)}, bf16[256,2048]{1,0:T(8,128)(2,1)}, u32[]{:S(2)}, u32[]{:S(2)}) collective-permute-start(bf16[256,2048]{1,0:T(8,128)(2,1)S(1)} %collective-permute-done.11), channel_id=1, source_target_pairs={{0,15},{1,0},{2,1},{3,2},{4,3},{5,4},{6,5},{7,6},{8,7},{9,8},{10,9... | collective-permute-start | bytes 3145736 | tf_op jit(solution)/shard_map/ppermute | solution.py:18
  129.8 20.9 %collective-permute-start.13 = (bf16[256,2048]{1,0:T(8,128)(2,1)}, bf16[256,2048]{1,0:T(8,128)(2,1)}, u32[]{:S(2)}, u32[]{:S(2)}) collective-permute-start(bf16[256,2048]{1,0:T(8,128)(2,1)} %collective-permute-done.12), channel_id=1, source_target_pairs={{0,15},{1,0},{2,1},{3,2},{4,3},{5,4},{6,5},{7,6},{8,7},{9,8},{10,9... | collective-permute-start | bytes 3145736 | tf_op jit(solution)/shard_map/ppermute | solution.py:18
  153.1 19.8 %all-to-all-start.3 = ((bf16[128,16,256]{0,2,1:T(8,128)(2,1)}), bf16[128,16,256]{0,2,1:T(8,128)(2,1)S(1)}, u32[]{:S(2)}, u32[]{:S(2)}) async-start(bf16[128,16,256]{0,2,1:T(8,128)(2,1)} %bitcast.224), calls=%async_computation.3 | async-start | bytes 2097152 | tf_op jit(solution)/shard_map/all_to_all | solution.py:138
  204.9 4.1 collective-permute-done.14
  215.8 5.7 all-to-all-start.1
  221.5 2.5 constant_dynamic-update-slice_fusion.12
  235.3 11.0 %all-to-all-done.1 = bf16[128,16,256]{0,2,1:T(8,128)(2,1)S(1)} async-done(((bf16[128,16,256]{0,2,1:T(8,128)(2,1)}), bf16[128,16,256]{0,2,1:T(8,128)(2,1)S(1)}, u32[]{:S(2)}, u32[]{:S(2)}) %all-to-all-start.1) | async-done | bytes 1048608 | tf_op jit(solution)/shard_map/all_to_all | solution.py:139
  246.3 4.9 all-to-all-start.2
  261.7 9.2 %fusion.11 = bf16[4096,128]{1,0:T(8,128)(2,1)} fusion(bf16[128,2048]{1,0:T(8,128)(2,1)S(1)} %copy-done, bf16[8192,2048]{1,0:T(8,128)(2,1)} %constant_dynamic-update-slice_fusion, s32[]{:T(128)S(6)} %select_n.152), kind=kOutput, calls=%fused_computation.15 | convolution fusion | flops 2148007936 | bytes 18350084 | tf_op jit(solution)/shard_map/tj,cj->tc/dot_general | solution.py:131
  271.0 5.2 all-to-all-done.2
  276.1 5.3 all-to-all-start
  285.3 5.6 copy.102
  293.4 5.6 copy.104
  301.0 5.7 fusion.31
  309.6 3.4 fusion.29
  313.1 6.3 %multiply_subtract_fusion.3 = (f32[1,32,256,128]{3,1,2,0:T(8,128)}, f32[1,32,256,128]{3,1,2,0:T(8,128)}, f32[1,32,256,128]{3,1,2,0:T(8,128)S(1)}, f32[1,32,256,128]{3,1,2,0:T(8,128)}) fusion(f32[2,32,256,128]{3,1,2,0:T(8,128)S(1)} %bitcast.213, f32[32,128]{1,0:T(8,128)S(1)} %copy-done.42, f32[32,128]{1,0:T(8,128)S(1)} %get-tuple-element.50, ...), kind=kLoop, calls=%fused_computation.25 | loop fusion | flops 12582912 | bytes 33587200 | tf_op jit(solution)/shard_map/sub | solution.py:39
  319.4 4.5 pad_maximum_fusion
  323.9 12.6 %fusion.14 = f32[2,32,256,128]{2,3,1,0:T(8,128)S(1)} fusion(f32[2,32,256,128]{3,1,2,0:T(8,128)S(1)} %pad_maximum_fusion, f32[1,2,128,128]{3,2,1,0:T(8,128)S(1)} %copy-done.33, f32[1,2,128,128]{3,2,1,0:T(8,128)S(1)} %copy-done.35), kind=kOutput, calls=%fused_computation.26 | convolution fusion | flops 6442516480 | bytes 17039360 | tf_op jit(solution)/shard_map/qzcn,pqkn->pzck/dot_general | solution.py:51
  336.5 3.2 pad_maximum_fusion.1
  339.7 16.8 %fusion.17 = f32[2,32,256,128]{2,3,1,0:T(8,128)} fusion(f32[2,32,256,128]{3,1,2,0:T(8,128)S(1)} %pad_maximum_fusion.1, f32[1,2,128,128]{3,2,1,0:T(8,128)S(1)} %copy-done.33, f32[1,2,128,128]{3,2,1,0:T(8,128)S(1)} %copy-done.35), kind=kOutput, calls=%fused_computation.27 | convolution fusion | flops 6442516480 | bytes 17039360 | tf_op jit(solution)/shard_map/qzcn,pqkn->pzck/dot_general | solution.py:51
  356.5 10.3 %multiply_add_fusion = (f32[1,32,256,128]{2,3,1,0:T(8,128)}, f32[1,32,256,128]{2,3,1,0:T(8,128)}, f32[1,32,256,128]{2,3,1,0:T(8,128)}, f32[1,32,256,128]{2,3,1,0:T(8,128)}) fusion(f32[2,32,256,128]{2,3,1,0:T(8,128)} %fusion.17, f32[2,32,256,128]{2,3,1,0:T(8,128)S(1)} %fusion.14, f32[1,32,256,128]{2,3,1,0:T(8,128)} %copy.104, f32[1,32,256,128]{2,3,1,0:T(8,128)S(1)} %copy-done.2), kind=kLoop, calls=%fused_computation.17 | loop fusion | flops 20971520 | bytes 41943040 | tf_op jit(solution)/shard_map/add | solution.py:116
  366.8 7.8 %maximum_bitcast_fusion = f32[2,32,256,128,1]{2,3,1,0,4:T(8,128)} fusion(f32[1,32,256,128]{2,3,1,0:T(8,128)} %get-tuple-element.20, f32[1,32,256,128]{2,3,1,0:T(8,128)} %get-tuple-element.21), kind=kLoop, calls=%fused_computation.4 | loop fusion | flops 2097152 | bytes 16777216 | tf_op jit(solution)/shard_map/stack | solution.py:110
  374.6 10.4 %copy.137 = f32[2,32,256,128,1]{3,1,0,2,4:T(8,128)} copy(f32[2,32,256,128,1]{2,3,1,0,4:T(8,128)} %maximum_bitcast_fusion) | data formatting | bytes 16777216 | tf_op jit(solution)/shard_map/stack | solution.py:110
  385.0 12.5 %convolution_bitcast_fusion = f32[2,32,256,128]{3,1,2,0:T(8,128)S(1)} fusion(f32[2,32,256,128,1]{3,1,0,2,4:T(8,128)} %copy.137, f32[1,2,128,128]{3,2,1,0:T(8,128)S(1)} %copy-done.38, f32[1,2,128,128]{3,2,1,0:T(8,128)S(1)} %copy-done.36), kind=kOutput, calls=%fused_computation.28 | convolution fusion | flops 6442516480 | bytes 17039360 | tf_op jit(solution)/shard_map/qzcn,pqkn->pzck/dot_general | solution.py:51
  398.9 5.0 fusion.20
  403.9 5.3 fusion.23
  411.2 6.0 %all-to-all-start.4 = ((f32[16,128,256]{1,2,0:T(8,128)}), f32[16,128,256]{1,2,0:T(8,128)S(1)}, u32[]{:S(2)}, u32[]{:S(2)}) async-start(f32[16,128,256]{1,2,0:T(8,128)} %copy.118), calls=%async_computation.4 | async-start | bytes 4194304 | tf_op jit(solution)/shard_map/all_to_all | solution.py:148
  417.2 3.6 copy.119
  420.8 43.8 %all-to-all-done.4 = f32[16,128,256]{1,2,0:T(8,128)S(1)} async-done(((f32[16,128,256]{1,2,0:T(8,128)}), f32[16,128,256]{1,2,0:T(8,128)S(1)}, u32[]{:S(2)}, u32[]{:S(2)}) %all-to-all-start.4) | async-done | bytes 2097184 | tf_op jit(solution)/shard_map/all_to_all | solution.py:148
  464.6 4.9 all-to-all-start.5
  469.5 3.7 copy.120
  473.2 43.9 %all-to-all-done.5 = f32[16,128,256]{1,2,0:T(8,128)} async-done(((f32[16,128,256]{1,2,0:T(8,128)}), f32[16,128,256]{1,2,0:T(8,128)}, u32[]{:S(2)}, u32[]{:S(2)}) %all-to-all-start.5) | async-done | bytes 2097184 | tf_op jit(solution)/shard_map/all_to_all | solution.py:149
  517.0 5.3 all-to-all-start.6
  522.3 5.6 copy.123
  528.0 2.9 reduce_sum.19
  531.0 5.6 copy.121
  536.6 2.9 reduce_sum.18
  543.3 2.9 copy.127
  546.2 23.5 %all-to-all-done.6 = f32[16,128,256]{1,2,0:T(8,128)} async-done(((f32[16,128,256]{1,2,0:T(8,128)}), f32[16,128,256]{1,2,0:T(8,128)}, u32[]{:S(2)}, u32[]{:S(2)}) %all-to-all-start.6) | async-done | bytes 2097184 | tf_op jit(solution)/shard_map/all_to_all | solution.py:156
  569.7 2.9 copy.128
  (203 shorter events, 92.2 us)
Async XLA Ops:
  0.6 261.1 %copy-start = (bf16[128,2048]{1,0:T(8,128)(2,1)S(1)}, bf16[128,2048]{1,0:T(8,128)(2,1)}, u32[]{:S(2)}) copy-start(bf16[128,2048]{1,0:T(8,128)(2,1)} %param.9) | copy-start | bytes 1572868
  0.6 176.7 %copy-start.45 = (f32[16,2048]{1,0:T(8,128)S(1)}, f32[16,2048]{1,0:T(8,128)}, u32[]{:S(2)}) copy-start(f32[16,2048]{1,0:T(8,128)} %param.11) | copy-start | bytes 393220
  0.7 13.9 %collective-permute-start = (bf16[256,2048]{1,0:T(8,128)(2,1)}, bf16[256,2048]{1,0:T(8,128)(2,1)S(1)}, u32[]{:S(2)}, u32[]{:S(2)}) collective-permute-start(bf16[256,2048]{1,0:T(8,128)(2,1)} %param.10), channel_id=1, source_target_pairs={{0,1},{1,2},{2,3},{3,4},{4,5},{5,6},{6,7},{7,8},{8,9},{9,10},{10,1... | collective-permute-start | bytes 3145736 | tf_op jit(solution)/shard_map/ppermute | solution.py:16
  14.6 179.2 %copy-start.9 = (bf16[256,2048]{1,0:T(8,128)(2,1)}, bf16[256,2048]{1,0:T(8,128)(2,1)S(1)}, u32[]{:S(2)}) copy-start(bf16[256,2048]{1,0:T(8,128)(2,1)S(1)} %collective-permute-done) | copy-start | bytes 3145732
  14.6 15.1 %collective-permute-start.1 = (bf16[256,2048]{1,0:T(8,128)(2,1)S(1)}, bf16[256,2048]{1,0:T(8,128)(2,1)S(1)}, u32[]{:S(2)}, u32[]{:S(2)}) collective-permute-start(bf16[256,2048]{1,0:T(8,128)(2,1)S(1)} %collective-permute-done), channel_id=1, source_target_pairs={{0,1},{1,2},{2,3},{3,4},{4,5},{5,6},{6,7},{7,8},{8,9},{9,10},{10,1... | collective-permute-start | bytes 3145736 | tf_op jit(solution)/shard_map/ppermute | solution.py:16
  17.8 15.4 %collective-permute-start.8 = (bf16[256,2048]{1,0:T(8,128)(2,1)}, bf16[256,2048]{1,0:T(8,128)(2,1)S(1)}, u32[]{:S(2)}, u32[]{:S(2)}) collective-permute-start(bf16[256,2048]{1,0:T(8,128)(2,1)} %param.10), channel_id=1, source_target_pairs={{0,15},{1,0},{2,1},{3,2},{4,3},{5,4},{6,5},{7,6},{8,7},{9,8},{10,9... | collective-permute-start | bytes 3145736 | tf_op jit(solution)/shard_map/ppermute | solution.py:18
  29.6 26.1 %copy-start.14 = (bf16[256,2048]{1,0:T(8,128)(2,1)}, bf16[256,2048]{1,0:T(8,128)(2,1)S(1)}, u32[]{:S(2)}) copy-start(bf16[256,2048]{1,0:T(8,128)(2,1)S(1)} %collective-permute-done.1) | copy-start | bytes 3145732
  29.6 23.8 %collective-permute-start.2 = (bf16[256,2048]{1,0:T(8,128)(2,1)S(1)}, bf16[256,2048]{1,0:T(8,128)(2,1)S(1)}, u32[]{:S(2)}, u32[]{:S(2)}) collective-permute-start(bf16[256,2048]{1,0:T(8,128)(2,1)S(1)} %collective-permute-done.1), channel_id=1, source_target_pairs={{0,1},{1,2},{2,3},{3,4},{4,5},{5,6},{6,7},{7,8},{8,9},{9,10},{10,1... | collective-permute-start | bytes 3145736 | tf_op jit(solution)/shard_map/ppermute | solution.py:16
  34.3 21.4 %collective-permute-start.9 = (bf16[256,2048]{1,0:T(8,128)(2,1)S(1)}, bf16[256,2048]{1,0:T(8,128)(2,1)S(1)}, u32[]{:S(2)}, u32[]{:S(2)}) collective-permute-start(bf16[256,2048]{1,0:T(8,128)(2,1)S(1)} %collective-permute-done.8), channel_id=1, source_target_pairs={{0,15},{1,0},{2,1},{3,2},{4,3},{5,4},{6,5},{7,6},{8,7},{9,8},{10,9... | collective-permute-start | bytes 3145736 | tf_op jit(solution)/shard_map/ppermute | solution.py:18
  53.4 52.2 %copy-start.21 = (bf16[256,2048]{1,0:T(8,128)(2,1)}, bf16[256,2048]{1,0:T(8,128)(2,1)S(1)}, u32[]{:S(2)}) copy-start(bf16[256,2048]{1,0:T(8,128)(2,1)S(1)} %collective-permute-done.2) | copy-start | bytes 3145732
  53.4 23.5 %collective-permute-start.3 = (bf16[256,2048]{1,0:T(8,128)(2,1)S(1)}, bf16[256,2048]{1,0:T(8,128)(2,1)S(1)}, u32[]{:S(2)}, u32[]{:S(2)}) collective-permute-start(bf16[256,2048]{1,0:T(8,128)(2,1)S(1)} %collective-permute-done.2), channel_id=1, source_target_pairs={{0,1},{1,2},{2,3},{3,4},{4,5},{5,6},{6,7},{7,8},{8,9},{9,10},{10,1... | collective-permute-start | bytes 3145736 | tf_op jit(solution)/shard_map/ppermute | solution.py:16
  55.7 21.2 %copy-start.16 = (bf16[256,2048]{1,0:T(8,128)(2,1)}, bf16[256,2048]{1,0:T(8,128)(2,1)S(1)}, u32[]{:S(2)}) copy-start(bf16[256,2048]{1,0:T(8,128)(2,1)S(1)} %collective-permute-done.9) | copy-start | bytes 3145732
  55.7 24.0 %collective-permute-start.10 = (bf16[256,2048]{1,0:T(8,128)(2,1)S(1)}, bf16[256,2048]{1,0:T(8,128)(2,1)S(1)}, u32[]{:S(2)}, u32[]{:S(2)}) collective-permute-start(bf16[256,2048]{1,0:T(8,128)(2,1)S(1)} %collective-permute-done.9), channel_id=1, source_target_pairs={{0,15},{1,0},{2,1},{3,2},{4,3},{5,4},{6,5},{7,6},{8,7},{9,8},{10,9... | collective-permute-start | bytes 3145736 | tf_op jit(solution)/shard_map/ppermute | solution.py:18
  76.9 52.9 %copy-start.25 = (bf16[256,2048]{1,0:T(8,128)(2,1)}, bf16[256,2048]{1,0:T(8,128)(2,1)S(1)}, u32[]{:S(2)}) copy-start(bf16[256,2048]{1,0:T(8,128)(2,1)S(1)} %collective-permute-done.3) | copy-start | bytes 3145732
  76.9 26.4 %collective-permute-start.4 = (bf16[256,2048]{1,0:T(8,128)(2,1)S(1)}, bf16[256,2048]{1,0:T(8,128)(2,1)S(1)}, u32[]{:S(2)}, u32[]{:S(2)}) collective-permute-start(bf16[256,2048]{1,0:T(8,128)(2,1)S(1)} %collective-permute-done.3), channel_id=1, source_target_pairs={{0,1},{1,2},{2,3},{3,4},{4,5},{5,6},{6,7},{7,8},{8,9},{9,10},{10,1... | collective-permute-start | bytes 3145736 | tf_op jit(solution)/shard_map/ppermute | solution.py:16
  80.7 24.9 %collective-permute-start.11 = (bf16[256,2048]{1,0:T(8,128)(2,1)S(1)}, bf16[256,2048]{1,0:T(8,128)(2,1)S(1)}, u32[]{:S(2)}, u32[]{:S(2)}) collective-permute-start(bf16[256,2048]{1,0:T(8,128)(2,1)S(1)} %collective-permute-done.10), channel_id=1, source_target_pairs={{0,15},{1,0},{2,1},{3,2},{4,3},{5,4},{6,5},{7,6},{8,7},{9,8},{10,9... | collective-permute-start | bytes 3145736 | tf_op jit(solution)/shard_map/ppermute | solution.py:18
  103.3 47.4 %copy-start.27 = (bf16[256,2048]{1,0:T(8,128)(2,1)}, bf16[256,2048]{1,0:T(8,128)(2,1)S(1)}, u32[]{:S(2)}) copy-start(bf16[256,2048]{1,0:T(8,128)(2,1)S(1)} %collective-permute-done.4) | copy-start | bytes 3145732
  103.3 24.1 %collective-permute-start.5 = (bf16[256,2048]{1,0:T(8,128)(2,1)S(1)}, bf16[256,2048]{1,0:T(8,128)(2,1)S(1)}, u32[]{:S(2)}, u32[]{:S(2)}) collective-permute-start(bf16[256,2048]{1,0:T(8,128)(2,1)S(1)} %collective-permute-done.4), channel_id=1, source_target_pairs={{0,1},{1,2},{2,3},{3,4},{4,5},{5,6},{6,7},{7,8},{8,9},{9,10},{10,1... | collective-permute-start | bytes 3145736 | tf_op jit(solution)/shard_map/ppermute | solution.py:16
  105.6 21.8 %copy-start.23 = (bf16[256,2048]{1,0:T(8,128)(2,1)}, bf16[256,2048]{1,0:T(8,128)(2,1)S(1)}, u32[]{:S(2)}) copy-start(bf16[256,2048]{1,0:T(8,128)(2,1)S(1)} %collective-permute-done.11) | copy-start | bytes 3145732
  105.6 24.2 %collective-permute-start.12 = (bf16[256,2048]{1,0:T(8,128)(2,1)S(1)}, bf16[256,2048]{1,0:T(8,128)(2,1)}, u32[]{:S(2)}, u32[]{:S(2)}) collective-permute-start(bf16[256,2048]{1,0:T(8,128)(2,1)S(1)} %collective-permute-done.11), channel_id=1, source_target_pairs={{0,15},{1,0},{2,1},{3,2},{4,3},{5,4},{6,5},{7,6},{8,7},{9,8},{10,9... | collective-permute-start | bytes 3145736 | tf_op jit(solution)/shard_map/ppermute | solution.py:18
  127.4 23.3 %copy-start.28 = (bf16[256,2048]{1,0:T(8,128)(2,1)}, bf16[256,2048]{1,0:T(8,128)(2,1)S(1)}, u32[]{:S(2)}) copy-start(bf16[256,2048]{1,0:T(8,128)(2,1)S(1)} %collective-permute-done.5) | copy-start | bytes 3145732
  127.4 23.3 %collective-permute-start.6 = (bf16[256,2048]{1,0:T(8,128)(2,1)S(1)}, bf16[256,2048]{1,0:T(8,128)(2,1)}, u32[]{:S(2)}, u32[]{:S(2)}) collective-permute-start(bf16[256,2048]{1,0:T(8,128)(2,1)S(1)} %collective-permute-done.5), channel_id=1, source_target_pairs={{0,1},{1,2},{2,3},{3,4},{4,5},{5,6},{6,7},{7,8},{8,9},{9,10},{10,1... | collective-permute-start | bytes 3145736 | tf_op jit(solution)/shard_map/ppermute | solution.py:16
  129.8 50.7 %collective-permute-start.13 = (bf16[256,2048]{1,0:T(8,128)(2,1)}, bf16[256,2048]{1,0:T(8,128)(2,1)}, u32[]{:S(2)}, u32[]{:S(2)}) collective-permute-start(bf16[256,2048]{1,0:T(8,128)(2,1)} %collective-permute-done.12), channel_id=1, source_target_pairs={{0,15},{1,0},{2,1},{3,2},{4,3},{5,4},{6,5},{7,6},{8,7},{9,8},{10,9... | collective-permute-start | bytes 3145736 | tf_op jit(solution)/shard_map/ppermute | solution.py:18
  150.8 30.2 %collective-permute-start.7 = (bf16[256,2048]{1,0:T(8,128)(2,1)}, bf16[256,2048]{1,0:T(8,128)(2,1)}, u32[]{:S(2)}, u32[]{:S(2)}) collective-permute-start(bf16[256,2048]{1,0:T(8,128)(2,1)} %collective-permute-done.6), channel_id=1, source_target_pairs={{0,1},{1,2},{2,3},{3,4},{4,5},{5,6},{6,7},{7,8},{8,9},{9,10},{10,1... | collective-permute-start | bytes 3145736 | tf_op jit(solution)/shard_map/ppermute | solution.py:16
  153.1 62.7 %all-to-all-start.3 = ((bf16[128,16,256]{0,2,1:T(8,128)(2,1)}), bf16[128,16,256]{0,2,1:T(8,128)(2,1)S(1)}, u32[]{:S(2)}, u32[]{:S(2)}) async-start(bf16[128,16,256]{0,2,1:T(8,128)(2,1)} %bitcast.224), calls=%async_computation.3 | async-start | bytes 2097152 | tf_op jit(solution)/shard_map/all_to_all | solution.py:138
  178.0 13.5 %copy-start.22 = (bf16[256,2048]{1,0:T(8,128)(2,1)S(1)}, bf16[256,2048]{1,0:T(8,128)(2,1)}, u32[]{:S(2)}) copy-start(bf16[256,2048]{1,0:T(8,128)(2,1)} %copy-done.21) | copy-start | bytes 3145732
  178.1 14.6 %copy-start.15 = (bf16[256,2048]{1,0:T(8,128)(2,1)S(1)}, bf16[256,2048]{1,0:T(8,128)(2,1)}, u32[]{:S(2)}) copy-start(bf16[256,2048]{1,0:T(8,128)(2,1)} %copy-done.14) | copy-start | bytes 3145732
  178.1 16.7 %copy-start.46 = (f32[32,32]{1,0:T(8,128)}, f32[32,32]{1,0:T(8,128)S(1)}, u32[]{:S(2)}) copy-start(f32[32,32]{1,0:T(8,128)S(1)} %fusion.79) | copy-start | bytes 12292
  178.2 16.6 %copy-start.48 = (f32[32,32]{1,0:T(8,128)}, f32[32,32]{1,0:T(8,128)S(1)}, u32[]{:S(2)}) copy-start(f32[32,32]{1,0:T(8,128)S(1)} %fusion.80) | copy-start | bytes 12292
  180.5 14.3 %copy-start.7 = (bf16[256,2048]{1,0:T(8,128)(2,1)S(1)}, bf16[256,2048]{1,0:T(8,128)(2,1)}, u32[]{:S(2)}) copy-start(bf16[256,2048]{1,0:T(8,128)(2,1)} %param.10) | copy-start | bytes 3145732
  180.6 28.4 %collective-permute-start.14 = (bf16[256,2048]{1,0:T(8,128)(2,1)}, bf16[256,2048]{1,0:T(8,128)(2,1)S(1)}, u32[]{:S(2)}, u32[]{:S(2)}) collective-permute-start(bf16[256,2048]{1,0:T(8,128)(2,1)} %collective-permute-done.13), channel_id=1, source_target_pairs={{0,15},{1,0},{2,1},{3,2},{4,3},{5,4},{6,5},{7,6},{8,7},{9,8},{10,9... | collective-permute-start | bytes 3145736 | tf_op jit(solution)/shard_map/ppermute | solution.py:18
  197.0 17.7 %copy-start.29 = (bf16[256,2048]{1,0:T(8,128)(2,1)S(1)}, bf16[256,2048]{1,0:T(8,128)(2,1)}, u32[]{:S(2)}) copy-start(bf16[256,2048]{1,0:T(8,128)(2,1)} %copy-done.28) | copy-start | bytes 3145732
  215.8 18.5 %copy-start.5 = (bf16[128,16,256]{0,2,1:T(8,128)(2,1)}, bf16[128,16,256]{0,2,1:T(8,128)(2,1)S(1)}, u32[]{:S(2)}) copy-start(bf16[128,16,256]{0,2,1:T(8,128)(2,1)S(1)} %all-to-all-done.3) | copy-start | bytes 3145732
  215.8 30.5 %all-to-all-start.1 = ((bf16[128,16,256]{0,2,1:T(8,128)(2,1)}), bf16[128,16,256]{0,2,1:T(8,128)(2,1)S(1)}, u32[]{:S(2)}, u32[]{:S(2)}) async-start(bf16[128,16,256]{0,2,1:T(8,128)(2,1)} %bitcast.225), calls=%async_computation.1 | async-start | bytes 2097152 | tf_op jit(solution)/shard_map/all_to_all | solution.py:139
  221.5 12.8 %copy-start.18 = (bf16[256,2048]{1,0:T(8,128)(2,1)S(1)}, bf16[256,2048]{1,0:T(8,128)(2,1)}, u32[]{:S(2)}) copy-start(bf16[256,2048]{1,0:T(8,128)(2,1)} %copy-done.16) | copy-start | bytes 3145732
  246.3 29.8 %all-to-all-start.2 = ((bf16[128,16,256]{0,2,1:T(8,128)(2,1)}), bf16[128,16,256]{0,2,1:T(8,128)(2,1)S(1)}, u32[]{:S(2)}, u32[]{:S(2)}) async-start(bf16[128,16,256]{0,2,1:T(8,128)(2,1)} %bitcast.223), calls=%async_computation.2 | async-start | bytes 2097152 | tf_op jit(solution)/shard_map/all_to_all | solution.py:140
  261.7 19.7 %copy-start.40 = (f32[2,8,16,128]{3,2,1,0:T(8,128)S(1)}, f32[2,8,16,128]{3,2,1,0:T(8,128)}, u32[]{:S(2)}) copy-start(f32[2,8,16,128]{3,2,1,0:T(8,128)} %copy.152) | copy-start | bytes 393220
  261.7 20.3 %copy-start.41 = (f32[32,128]{1,0:T(8,128)S(1)}, f32[32,128]{1,0:T(8,128)}, u32[]{:S(2)}) copy-start(f32[32,128]{1,0:T(8,128)} %get-tuple-element.49) | copy-start | bytes 49156
  261.7 20.4 %copy-start.32 = (f32[1,2,128,128]{3,2,1,0:T(8,128)S(1)}, f32[1,2,128,128]{3,2,1,0:T(8,128)}, u32[]{:S(2)}) copy-start(f32[1,2,128,128]{3,2,1,0:T(8,128)} %get-tuple-element.38) | copy-start | bytes 393220
  261.7 20.4 %copy-start.34 = (f32[1,2,128,128]{3,2,1,0:T(8,128)S(1)}, f32[1,2,128,128]{3,2,1,0:T(8,128)}, u32[]{:S(2)}) copy-start(f32[1,2,128,128]{3,2,1,0:T(8,128)} %get-tuple-element.39) | copy-start | bytes 393220
  276.1 23.1 %copy-start.3 = (bf16[128,16,256]{0,2,1:T(8,128)(2,1)}, bf16[128,16,256]{0,2,1:T(8,128)(2,1)S(1)}, u32[]{:S(2)}) copy-start(bf16[128,16,256]{0,2,1:T(8,128)(2,1)S(1)} %all-to-all-done.2) | copy-start | bytes 3145732
  276.1 30.5 %all-to-all-start = ((bf16[128,16,256]{0,2,1:T(8,128)(2,1)}), bf16[128,16,256]{0,2,1:T(8,128)(2,1)}, u32[]{:S(2)}, u32[]{:S(2)}) async-start(bf16[128,16,256]{0,2,1:T(8,128)(2,1)} %bitcast.228), calls=%async_computation | async-start | bytes 2097152 | tf_op jit(solution)/shard_map/all_to_all | solution.py:141
  299.1 98.3 %copy-start.43 = (f32[32,128]{1,0:T(8,128)}, f32[32,128]{1,0:T(8,128)S(1)}, u32[]{:S(2)}) copy-start(f32[32,128]{1,0:T(8,128)S(1)} %broadcast_multiply_fusion.1) | copy-start | bytes 49156
  339.7 16.8 %copy-start.2 = (f32[1,32,256,128]{2,3,1,0:T(8,128)S(1)}, f32[1,32,256,128]{2,3,1,0:T(8,128)}, u32[]{:S(2)}) copy-start(f32[1,32,256,128]{2,3,1,0:T(8,128)} %copy.102) | copy-start | bytes 12582916
  411.2 53.4 %all-to-all-start.4 = ((f32[16,128,256]{1,2,0:T(8,128)}), f32[16,128,256]{1,2,0:T(8,128)S(1)}, u32[]{:S(2)}, u32[]{:S(2)}) async-start(f32[16,128,256]{1,2,0:T(8,128)} %copy.118), calls=%async_computation.4 | async-start | bytes 4194304 | tf_op jit(solution)/shard_map/all_to_all | solution.py:148
  464.6 52.4 %all-to-all-start.5 = ((f32[16,128,256]{1,2,0:T(8,128)}), f32[16,128,256]{1,2,0:T(8,128)}, u32[]{:S(2)}, u32[]{:S(2)}) async-start(f32[16,128,256]{1,2,0:T(8,128)} %copy.119), calls=%async_computation.5 | async-start | bytes 4194304 | tf_op jit(solution)/shard_map/all_to_all | solution.py:149
  517.0 52.7 %all-to-all-start.6 = ((f32[16,128,256]{1,2,0:T(8,128)}), f32[16,128,256]{1,2,0:T(8,128)}, u32[]{:S(2)}, u32[]{:S(2)}) async-start(f32[16,128,256]{1,2,0:T(8,128)} %copy.120), calls=%async_computation.6 | async-start | bytes 4194304 | tf_op jit(solution)/shard_map/all_to_all | solution.py:156
  536.6 36.0 %copy-start.1 = (bf16[128,2048]{1,0:T(8,128)(2,1)S(1)}, bf16[128,2048]{1,0:T(8,128)(2,1)}, u32[]{:S(2)}) copy-start(bf16[128,2048]{1,0:T(8,128)(2,1)} %param.9) | copy-start | bytes 1572868
  (30 other events, 238.3 us)
